TPU v7x, 32 devices: a whole 2x2x4 slice. The times are simulated.
32 devices in a mesh: wheel: 16 (over z, x, core), slab: 2 (over y).
Axes of the slice: x: 2, y: 2, z: 4, core: 2. Of those that a mesh axis runs over, the one named last changes fastest.
Arguments:
- krylov_block: float32 [2, 32, 3, 16, 512], P(None, 'wheel', None, None, 'slab'), may hold values from -6 to 6
- blade_class: int32 [32], P('wheel'), may hold values from 0 to 3
- neighbors: int32 [8, 512], P(None, 'slab'), may hold values from 0 to 511
- iface_rows: int32 [2, 128], P(None, 'slab'), may hold values from 0 to 255
- face_rows: int32 [2, 128], P(None, 'slab'), may hold values from 0 to 255
- stiffness: float32 [3, 3, 8, 512], P(None, None, None, 'slab'), may hold values from -1.25 to 1.25
- lumped_mass: float32 [3, 512], P(None, 'slab'), may hold values from 0.5 to 2
- precond: bfloat16 [16, 16, 384, 384], P('wheel', 'slab'), may hold values from -0.3125 to 0.3125
Outputs:
- preconditioned: float32 [16, 16, 16, 384], P('wheel', 'slab')
Inputs may be any that keep to these rules, and one draw needn't show every extreme that they name: `neighbors`: extended numbering: own nodes first (256), then 64 from the lower slab, 64 from the upper slab, 64 from the previous sector, 64 from the next sector.
All inputs are finite; a program needn't handle non-finite values.
Results may differ from a plain program's by a relative error of at most 0.0039.
Values may be sent and summed in bfloat16 or wider, within the bound.
No kernel may reach another device: no remote copies, remote signals or barrier semaphores. Data moves between devices by JAX's collectives and lax.ppermute only.
A program may use at most 64 MiB of HBM per device.

v0:
```python
import math
import jax
import jax.numpy as jnp
from jax import lax
from jax.sharding import PartitionSpec as P

GROUP = 32
damping_ratio = 0.5
gyro_rate = 0.8
shift_value = 0.3
class_step = 0.125


def extended_2(block, sides, width, periodic):
    for axis, dim in sides:
        count = lax.axis_size(axis)
        forward = [(i, i + 1) for i in range(count - 1)]
        if periodic:
            forward.append((count - 1, 0))
        backward = [(target, source) for source, target in forward]
        low = lax.ppermute(
            lax.slice_in_dim(block, block.shape[dim] - width, None, axis=dim), axis, forward
        )
        high = lax.ppermute(lax.slice_in_dim(block, 0, width, axis=dim), axis, backward)
        block = jnp.concatenate([low, block, high], axis=dim)
    return block


def basis(row_ids, col_ids, sectors_all):
    pair_id = row_ids[:, None] // 2
    part_id = row_ids[:, None] % 2
    sector_id = col_ids[None, :]
    phases = pair_id * sector_id % sectors_all
    angles = 2.0 * math.pi / sectors_all * phases.astype(jnp.float32)
    parity = (1 - 2 * (sector_id % 2)).astype(jnp.float32)
    edge_rows = jnp.where(
        part_id == 0, jnp.ones_like(angles), parity * jnp.ones_like(angles)
    ) * math.sqrt(1.0 / sectors_all)
    inner_rows = jnp.where(part_id == 0, jnp.cos(angles), jnp.sin(angles)) * math.sqrt(
        2.0 / sectors_all
    )
    return jnp.where(pair_id == 0, edge_rows, inner_rows)


def arrange(harmonic):
    pair_rows, states, comps, vectors, nodes = harmonic.shape
    shaped = harmonic.reshape(pair_rows // 2, 2, states, comps, vectors, nodes // GROUP, GROUP)
    shaped = shaped.transpose(0, 5, 4, 1, 2, 3, 6)
    return shaped.reshape(pair_rows // 2, nodes // GROUP, vectors, 4 * comps * GROUP)


def on_device(
    krylov_block, blade_class, neighbors, iface_rows, face_rows, stiffness, lumped_mass, precond
):
    displacement = krylov_block[0]
    velocity = krylov_block[1]
    moved_field = displacement + damping_ratio * velocity
    rim_width = iface_rows.shape[1]
    face_width = face_rows.shape[1]
    rims = jnp.concatenate(
        (
            jnp.take(moved_field, iface_rows[0], axis=3),
            jnp.take(moved_field, iface_rows[1], axis=3),
        ),
        axis=3,
    )
    rimmed = extended_2(rims.astype(jnp.bfloat16), (("slab", 3),), rim_width, False).astype(
        rims.dtype
    )
    from_lower = rimmed[..., :rim_width]
    from_upper = rimmed[..., 3 * rim_width :]
    left_face = jnp.take(moved_field, face_rows[0], axis=3)
    right_face = jnp.take(moved_field, face_rows[1], axis=3)
    edges = jnp.concatenate((left_face[0], right_face[-1]), axis=2)
    faced = extended_2(edges, (("wheel", 2),), face_width, True)
    from_prev = jnp.concatenate((faced[None, :, :, :face_width], right_face[:-1]), axis=0)
    from_next = jnp.concatenate((left_face[1:], faced[None, :, :, 3 * face_width :]), axis=0)
    extended = jnp.concatenate((moved_field, from_lower, from_upper, from_prev, from_next), axis=3)
    picked = jnp.take(extended, neighbors, axis=3)
    restore = jnp.einsum("cdkn,sdvkn->scvn", stiffness, picked, precision=lax.Precision.HIGHEST)
    scale = (1.0 + class_step * blade_class.astype(jnp.float32))[:, None, None, None]
    gyro = gyro_rate * jnp.stack(
        (
            -lumped_mass[0] * velocity[:, 1],
            lumped_mass[1] * velocity[:, 0],
            jnp.zeros_like(velocity[:, 2]),
        ),
        axis=1,
    )
    res_disp = velocity - shift_value * displacement
    res_velo = -scale * restore - gyro - shift_value * lumped_mass[None, :, None, :] * velocity
    residual = jnp.stack((res_disp, res_velo), axis=0)
    local_sectors = residual.shape[1]
    sectors_all = lax.axis_size("wheel") * local_sectors
    spread = lax.all_to_all(residual, "wheel", split_axis=4, concat_axis=1, tiled=True)
    table = basis(
        jnp.arange(sectors_all, dtype=jnp.int32),
        jnp.arange(sectors_all, dtype=jnp.int32),
        sectors_all,
    )
    transformed = jnp.einsum(
        "bs,tscvn->btcvn", table, spread, precision=lax.Precision.HIGHEST
    ).astype(jnp.bfloat16)
    harmonic = lax.all_to_all(transformed, "wheel", split_axis=0, concat_axis=4, tiled=True)
    lhs = arrange(harmonic)
    return jnp.einsum("pgvj,pgij->pgvi", lhs, precond, preferred_element_type=jnp.float32)


def solution(mesh):
    return jax.shard_map(
        on_device,
        mesh=mesh,
        in_specs=(
            P(None, "wheel", None, None, "slab"),
            P("wheel"),
            P(None, "slab"),
            P(None, "slab"),
            P(None, "slab"),
            P(None, None, None, "slab"),
            P(None, "slab"),
            P("wheel", "slab", None, None),
        ),
        out_specs=P("wheel", "slab", None, None),
        check_vma=False,
    )
```

profile of v0, /device:TPU:0, one launch (start us, length us, event | category | flops | bytes accessed | tf_op | source)
XLA Modules:
  0.0 120.3 jit_solution(17209610336945923455)
XLA Ops:
  0.0 1.1 bitcast_add_fusion
  1.1 0.5 copy.155
  1.6 1.4 %compare_and_fusion.4 = (pred[64]{0:T(512)(128)(4,1)}, s32[64]{0:T(128)S(1)}, pred[64]{0:T(512)(128)(4,1)}, s32[64]{0:T(128)}) fusion(s32[2,64]{1,0:T(2,128)} %param.13), kind=kLoop, calls=%fused_computation.77 | loop fusion | flops 768 | bytes 1152 | tf_op jit(solution)/shard_map/jit(_take)/and | solution.py:63
  3.0 0.8 gather_fusion.1
  3.8 0.7 copy.156
  4.5 1.4 %bitcast_convert_fusion.1 = bf16[2,3,16,64]{3,2,1,0:T(8,128)(2,1)} fusion(bf16[64,2,3,16]{0,3,2,1:T(8,128)(2,1)} %copy.156, pred[64]{0:T(512)(128)(4,1)} %get-tuple-element.10), kind=kLoop, calls=%fused_computation.26 | loop fusion | flops 6144 | bytes 24640 | tf_op jit(solution)/shard_map/slice | solution.py:22
  5.9 5.5 %collective-permute-start = (bf16[2,3,16,64]{3,2,1,0:T(8,128)(2,1)}, bf16[2,3,16,64]{3,2,1,0:T(8,128)(2,1)}, u32[]{:S(2)}, u32[]{:S(2)}) collective-permute-start(bf16[2,3,16,64]{3,2,1,0:T(8,128)(2,1)} %bitcast_convert_fusion.1), channel_id=1, source_target_pairs={{0,1},{2,3},{4,5},{6,7},{8,9},{10,11},{12,13},{14,15},{16,17},{18,... | collective-permute-start | bytes 36872 | tf_op jit(solution)/shard_map/ppermute | solution.py:21
  11.3 0.7 pad_clamp_fusion.2
  12.0 0.8 gather_fusion.2
  12.9 0.7 copy.158
  13.6 1.3 %bitcast_convert_fusion = bf16[2,3,16,64]{3,2,1,0:T(8,128)(2,1)} fusion(bf16[64,2,3,16]{0,3,2,1:T(8,128)(2,1)} %copy.158, pred[64]{0:T(512)(128)(4,1)} %get-tuple-element.28), kind=kLoop, calls=%fused_computation.25 | loop fusion | flops 6144 | bytes 24640 | tf_op jit(solution)/shard_map/slice | solution.py:24
  14.9 1.3 %collective-permute-start.1 = (bf16[2,3,16,64]{3,2,1,0:T(8,128)(2,1)}, bf16[2,3,16,64]{3,2,1,0:T(8,128)(2,1)}, u32[]{:S(2)}, u32[]{:S(2)}) collective-permute-start(bf16[2,3,16,64]{3,2,1,0:T(8,128)(2,1)} %bitcast_convert_fusion), channel_id=1, source_target_pairs={{1,0},{3,2},{5,4},{7,6},{9,8},{11,10},{13,12},{15,14},{17,16},{19,... | collective-permute-start | bytes 36872 | tf_op jit(solution)/shard_map/ppermute | solution.py:24
  16.2 0.8 compare_and_fusion.1
  17.0 1.5 %gather_fusion.3 = f32[64,2,3,16]{3,1,2,0:T(2,128)} fusion(f32[2,3,16,256]{2,0,3,1:T(2,128)S(1)} %copy.155, s32[1024]{0:T(1024)S(1)} %pad_clamp_fusion.1), kind=kCustom, calls=%fused_computation.2.clone | custom fusion | bytes 49408 | tf_op jit(solution)/shard_map/jit(_take)/gather | solution.py:73
  18.5 1.0 copy.160
  19.5 1.5 %gather_fusion.4 = f32[64,2,3,16]{3,1,2,0:T(2,128)} fusion(f32[2,3,16,256]{2,0,3,1:T(2,128)S(1)} %copy.155, s32[1024]{0:T(1024)S(1)} %pad_clamp_fusion), kind=kCustom, calls=%fused_computation.3.clone | custom fusion | bytes 49408 | tf_op jit(solution)/shard_map/jit(_take)/gather | solution.py:72
  21.0 1.0 copy.162
  22.0 3.7 %collective-permute-start.3 = (f32[3,16,64]{2,1,0:T(8,128)S(1)}, f32[3,16,64]{2,1,0:T(8,128)S(1)}, u32[]{:S(2)}, u32[]{:S(2)}) collective-permute-start(f32[3,16,64]{2,1,0:T(8,128)S(1)} %get-tuple-element.21), channel_id=1, source_target_pairs={{2,0},{4,2},{6,4},{8,6},{10,8},{12,10},{14,12},{16,14},{18,16},{20... | collective-permute-start | bytes 36872 | tf_op jit(solution)/shard_map/ppermute | solution.py:24
  25.8 0.7 multiply_subtract_fusion
  26.5 0.6 slice_multiply_fusion.1
  27.2 0.7 add_negate_fusion
  27.8 2.2 %copy.173 = f32[3,3,8,256,1]{2,0,1,4,3:T(4,128)} copy(f32[3,3,8,256,1]{3,2,1,0,4:T(8,128)} %bitcast.88) | data formatting | bytes 147456 | tf_op args[5]
  30.3 0.9 maximum_convert_fusion
  31.3 0.5 collective-permute-done.2
  31.9 2.1 %copy.163 = f32[2,3,16,512]{2,0,3,1:T(2,128)} copy(f32[2,3,16,512]{3,2,1,0:T(8,128)S(1)} %concatenate.18) | data formatting | bytes 393216 | tf_op jit(solution)/shard_map/concatenate | solution.py:78
  33.9 23.2 %gather_fusion = f32[2048,2,3,16]{3,1,2,0:T(2,128)} fusion(f32[2,3,16,512]{2,0,3,1:T(2,128)} %copy.163, s32[2048]{0:T(1024)S(1)} %broadcast_clamp_fusion), kind=kCustom, calls=%fused_computation.4 | custom fusion | bytes 1581056 | tf_op jit(solution)/shard_map/jit(_take)/gather | solution.py:79
  57.1 10.7 %fusion.6 = f32[256,2,16,3]{2,3,1,0:T(4,128)S(1)} fusion(f32[3,3,8,256,1]{2,0,1,4,3:T(4,128)} %copy.173, f32[8,256,2,3,16]{4,2,3,1,0:T(2,128)} %bitcast.80, pred[8,256]{0,1:T(8,128)(4,1)S(1)} %copy.154), kind=kOutput, calls=%fused_computation.12 | convolution fusion | flops 7274496 | bytes 960512 | tf_op jit(solution)/shard_map/cdkn,sdvkn->scvn/dot_general | solution.py:80
  67.9 0.4 copy.166
  68.3 1.0 fusion.14
  69.3 0.9 pad_maximum_fusion
  70.2 2.2 %copy.167 = f32[2,2,3,16,256]{3,1,2,0,4:T(2,128)} copy(f32[2,2,3,16,256]{4,3,2,1,0:T(8,128)S(1)} %pad_maximum_fusion) | data formatting | bytes 393216 | tf_op jit(solution)/shard_map/stack | solution.py:92
  72.3 4.2 %reshape.174 = f32[16,1,3072]{2,1,0:T(1,128)} reshape(f32[256,2,3,2,16]{4,3,2,1,0:T(2,128)} %bitcast.81) | data formatting | bytes 393216
  76.6 5.4 %all-to-all-start = ((f32[16,1,3072]{2,1,0:T(1,128)}), f32[16,1,3072]{2,1,0:T(1,128)S(1)}, u32[]{:S(2)}, u32[]{:S(2)}) async-start(f32[16,1,3072]{2,1,0:T(1,128)} %reshape.174), calls=%async_computation | async-start | bytes 393216 | tf_op jit(solution)/shard_map/all_to_all | solution.py:95
  82.0 8.9 %all-to-all-done = f32[16,1,3072]{2,1,0:T(1,128)S(1)} async-done(((f32[16,1,3072]{2,1,0:T(1,128)}), f32[16,1,3072]{2,1,0:T(1,128)S(1)}, u32[]{:S(2)}, u32[]{:S(2)}) %all-to-all-start) | async-done | bytes 196640 | tf_op jit(solution)/shard_map/all_to_all | solution.py:95
  90.9 0.5 broadcast.231
  91.4 1.1 reduce
  92.5 3.3 %reshape.175 = f32[256,2,3,2,16]{4,3,2,1,0:T(2,128)} reshape(f32[16,3072]{1,0:T(8,128)S(1)} %reduce) | data formatting | bytes 393216
  95.8 3.7 %copy.168 = f32[2,2,3,16,16,16]{5,3,2,1,4,0:T(8,128)} copy(f32[2,2,3,16,16,16]{3,1,2,0,5,4:T(2,128)} %bitcast.82) | data formatting | bytes 393216 | tf_op jit(solution)/shard_map/all_to_all | solution.py:95
  99.5 2.0 %copy.169 = f32[2,32,3,16,16]{1,4,3,2,0:T(8,128)S(1)} copy(f32[2,32,3,16,16]{4,3,2,1,0:T(8,128)} %bitcast.83) | data formatting | bytes 393216 | tf_op jit(solution)/shard_map/all_to_all | solution.py:95
  101.4 0.9 fusion.18
  102.4 1.3 %copy.170 = bf16[32,2,3,16,16]{4,3,2,1,0:T(8,128)(2,1)S(1)} copy(bf16[32,2,3,16,16]{0,4,3,2,1:T(8,128)(2,1)S(1)} %convert_element_type.25) | data formatting | bytes 196608 | tf_op jit(solution)/shard_map/convert_element_type | solution.py:103
  103.7 0.8 reshape.176
  104.5 10.0 %all_to_all.33 = bf16[16,2,1536]{2,1,0:T(2,128)(2,1)S(1)} all-to-all(bf16[16,2,1536]{2,1,0:T(2,128)(2,1)S(1)} %reshape.176), channel_id=1, replica_groups=mesh['wheel'=16,'slab'=2] {'wheel'}, dimensions={0} | all-to-all | bytes 196608 | tf_op jit(solution)/shard_map/all_to_all | solution.py:104
  114.5 0.5 reshape.177
  115.0 1.4 %copy.171 = bf16[2,2,3,16,16,16]{5,4,3,2,1,0:T(8,128)(2,1)} copy(bf16[2,2,3,16,16,16]{5,3,2,1,0,4:T(8,128)(2,1)S(1)} %bitcast.85) | data formatting | bytes 196608 | tf_op jit(solution)/shard_map/all_to_all | solution.py:104
  116.4 1.7 %reshape.112 = bf16[1,2,2,3,16,8,32]{6,5,4,3,2,1,0:T(8,128)(2,1)S(1)} reshape(bf16[2,2,3,16,16,16]{5,4,3,2,1,0:T(8,128)(2,1)} %copy.171) | data formatting | bytes 196608 | tf_op jit(solution)/shard_map/reshape | solution.py:47
  118.1 0.3 copy.172
  118.8 1.5 %fusion.9 = f32[1,8,16,384]{3,2,1,0:T(8,128)} fusion(bf16[8,16,384]{2,1,0:T(8,128)(2,1)S(1)} %reshape.113, bf16[1,8,384,384]{3,2,1,0:T(8,128)(2,1)S(1)} %copy-done), kind=kOutput, calls=%fused_computation.13 | convolution fusion | flops 37748736 | bytes 2654208 | tf_op jit(solution)/shard_map/pgvj,pgij->pgvi/dot_general | solution.py:106
  (34 shorter events, 0.9 us)
Async XLA Ops:
  0.0 118.8 %copy-start = (bf16[1,8,384,384]{3,2,1,0:T(8,128)(2,1)S(1)}, bf16[1,8,384,384]{3,2,1,0:T(8,128)(2,1)}, u32[]{:S(2)}) copy-start(bf16[1,8,384,384]{3,2,1,0:T(8,128)(2,1)} %param.17) | copy-start | bytes 7077892
  0.0 25.8 %copy-start.1 = (f32[2,2,3,16,256]{4,3,2,1,0:T(8,128)S(1)}, f32[2,2,3,16,256]{4,3,2,1,0:T(8,128)}, u32[]{:S(2)}) copy-start(f32[2,2,3,16,256]{4,3,2,1,0:T(8,128)} %param.10) | copy-start | bytes 589828
  0.0 25.8 %copy-start.2 = (s32[8,256]{1,0:T(8,128)S(1)}, s32[8,256]{1,0:T(8,128)}, u32[]{:S(2)}) copy-start(s32[8,256]{1,0:T(8,128)} %param.12) | copy-start | bytes 24580
  0.0 26.5 %copy-start.3 = (f32[3,256]{1,0:T(4,128)S(1)}, f32[3,256]{1,0:T(4,128)}, u32[]{:S(2)}) copy-start(f32[3,256]{1,0:T(4,128)} %param.16) | copy-start | bytes 9220
  5.9 24.4 %collective-permute-start = (bf16[2,3,16,64]{3,2,1,0:T(8,128)(2,1)}, bf16[2,3,16,64]{3,2,1,0:T(8,128)(2,1)}, u32[]{:S(2)}, u32[]{:S(2)}) collective-permute-start(bf16[2,3,16,64]{3,2,1,0:T(8,128)(2,1)} %bitcast_convert_fusion.1), channel_id=1, source_target_pairs={{0,1},{2,3},{4,5},{6,7},{8,9},{10,11},{12,13},{14,15},{16,17},{18,... | collective-permute-start | bytes 36872 | tf_op jit(solution)/shard_map/ppermute | solution.py:21
  14.9 15.4 %collective-permute-start.1 = (bf16[2,3,16,64]{3,2,1,0:T(8,128)(2,1)}, bf16[2,3,16,64]{3,2,1,0:T(8,128)(2,1)}, u32[]{:S(2)}, u32[]{:S(2)}) collective-permute-start(bf16[2,3,16,64]{3,2,1,0:T(8,128)(2,1)} %bitcast_convert_fusion), channel_id=1, source_target_pairs={{1,0},{3,2},{5,4},{7,6},{9,8},{11,10},{13,12},{15,14},{17,16},{19,... | collective-permute-start | bytes 36872 | tf_op jit(solution)/shard_map/ppermute | solution.py:24
  22.0 9.2 %collective-permute-start.3 = (f32[3,16,64]{2,1,0:T(8,128)S(1)}, f32[3,16,64]{2,1,0:T(8,128)S(1)}, u32[]{:S(2)}, u32[]{:S(2)}) collective-permute-start(f32[3,16,64]{2,1,0:T(8,128)S(1)} %get-tuple-element.21), channel_id=1, source_target_pairs={{2,0},{4,2},{6,4},{8,6},{10,8},{12,10},{14,12},{16,14},{18,16},{20... | collective-permute-start | bytes 36872 | tf_op jit(solution)/shard_map/ppermute | solution.py:24
  25.8 5.9 %collective-permute-start.2 = (f32[3,16,64]{2,1,0:T(8,128)S(1)}, f32[3,16,64]{2,1,0:T(8,128)S(1)}, u32[]{:S(2)}, u32[]{:S(2)}) collective-permute-start(f32[3,16,64]{2,1,0:T(8,128)S(1)} %get-tuple-element.22), channel_id=1, source_target_pairs={{0,2},{2,4},{4,6},{6,8},{8,10},{10,12},{12,14},{14,16},{16,18},{18... | collective-permute-start | bytes 36872 | tf_op jit(solution)/shard_map/ppermute | solution.py:21
  76.6 14.3 %all-to-all-start = ((f32[16,1,3072]{2,1,0:T(1,128)}), f32[16,1,3072]{2,1,0:T(1,128)S(1)}, u32[]{:S(2)}, u32[]{:S(2)}) async-start(f32[16,1,3072]{2,1,0:T(1,128)} %reshape.174), calls=%async_computation | async-start | bytes 393216 | tf_op jit(solution)/shard_map/all_to_all | solution.py:95
where the time goes:
time: 121 us; the launch traced here: 120 us
  local copies, waits for them, and re-layouts  59 us (49%)
  starting transfers between devices  15.9 us (13%)
  matrix products  13.1 us (11%)
  other arithmetic  12.6 us (10%)
  blocking collectives  9.96 us (8%)
  waiting for transfers between devices  9.41 us (8%)
    gather x1, local copies, waits for them, and re-layouts, on_device(): picked = jnp.take(extended, neighbors, axis=3)  23.2 us
    unnamed x14, local copies, waits for them, and re-layouts  11.1 us
    dot_general x1, matrix products, on_device(): jnp.einsum('cdkn,sdvkn->scvn', stiffness, picked, precision=lax.Precision...  10.7 us
    all_to_all x1, blocking collectives, on_device(): lax.all_to_all(transformed, 'wheel', split_axis=0, concat_axis=4, tiled=T...  9.96 us
    all_to_all x1, waiting for transfers between devices, on_device(): lax.all_to_all(residual, 'wheel', split_axis=4, concat_axis=1, tiled=True)  8.93 us
    all_to_all x3, local copies, waits for them, and re-layouts, on_device(): lax.all_to_all(residual, 'wheel', split_axis=4, concat_axis=1, tiled=True)  6.2 us
    ppermute x2, starting transfers between devices, extended_2(): lax.ppermute(lax.slice_in_dim(block, block.shape[dim] - width, None, axis...  5.49 us
    all_to_all x1, starting transfers between devices, on_device(): lax.all_to_all(residual, 'wheel', split_axis=4, concat_axis=1, tiled=True)  5.36 us
  transfers between devices with their start and end apart: 5, of which 2 were waited for; matrix products, arithmetic and copies ran while one was open for 12% of the time, Pallas kernels for 0%

commit v1 on v0

--- a/solution.py
+++ b/solution.py
@@ -101,7 +101,14 @@
     transformed = jnp.einsum(
         "bs,tscvn->btcvn", table, spread, precision=lax.Precision.HIGHEST
     ).astype(jnp.bfloat16)
-    harmonic = lax.all_to_all(transformed, "wheel", split_axis=0, concat_axis=4, tiled=True)
+
+    def recover_the_quotas(vector, pos_dim, in_dim):
+        b_next = lax.all_to_all(
+            jnp.stack(jnp.split(vector, lax.axis_size("wheel"), axis=pos_dim)), "wheel", 0, 0
+        )
+        return jnp.concatenate(b_next, axis=in_dim)
+
+    harmonic = recover_the_quotas(transformed, 0, 4)
     lhs = arrange(harmonic)
     return jnp.einsum("pgvj,pgij->pgvi", lhs, precond, preferred_element_type=jnp.float32)
 

time: 121 us -> 180 us (1.49); the launches traced: 120 us -> 177 us
  local copies, waits for them, and re-layouts: 59 us -> 117 us
    another operation x1 -> x20, local copies, waits for them, and re-layouts: 0.32 us -> 39.1 us  [the longest x18 37.1 us: recover_the_quotas(): jnp.stack(jnp.split(vector, lax.axis_size('wheel'), axis=pos_dim))]
    unnamed x14 -> x29, local copies, waits for them, and re-layouts: 11.1 us -> 32.7 us
  transfers between devices with their start and end apart: 5 -> 5, of which waited for: 2 -> 1; matrix products, arithmetic and copies ran while one was open for 12% -> 9% of each run, Pallas kernels for 0% -> 0%
where the time goes in v1:
time: 180 us; the launch traced here: 177 us
  local copies, waits for them, and re-layouts  117 us (65%)
  starting transfers between devices  15 us (8%)
  other arithmetic  13.3 us (7%)
  matrix products  13.1 us (7%)
  blocking collectives  9.96 us (6%)
  waiting for transfers between devices  8.73 us (5%)
    another operation x18, local copies, waits for them, and re-layouts, recover_the_quotas(): jnp.stack(jnp.split(vector, lax.axis_size('wheel'), axis=pos_dim))  37.1 us
    unnamed x29, local copies, waits for them, and re-layouts  32.7 us
    gather x1, local copies, waits for them, and re-layouts, on_device(): picked = jnp.take(extended, neighbors, axis=3)  23.1 us
    dot_general x1, matrix products, on_device(): jnp.einsum('cdkn,sdvkn->scvn', stiffness, picked, precision=lax.Precision...  10.7 us
    all_to_all x1, blocking collectives, recover_the_quotas(): lax.all_to_all(jnp.stack(jnp.split(vector, lax.axis_size('wheel'), axis=p...  9.96 us
    all_to_all x1, waiting for transfers between devices, on_device(): lax.all_to_all(residual, 'wheel', split_axis=4, concat_axis=1, tiled=True)  8.72 us
    all_to_all x3, local copies, waits for them, and re-layouts, on_device(): lax.all_to_all(residual, 'wheel', split_axis=4, concat_axis=1, tiled=True)  6.21 us
    ppermute x2, starting transfers between devices, extended_2(): lax.ppermute(lax.slice_in_dim(block, 0, width, axis=dim), axis, backward)  5.77 us
  transfers between devices with their start and end apart: 5, of which 1 were waited for; matrix products, arithmetic and copies ran while one was open for 9% of the time, Pallas kernels for 0%

profile of v1, /device:TPU:0, one launch (start us, length us, event | category | flops | bytes accessed | tf_op | source)
XLA Modules:
  0.0 177.3 jit_solution(11596601320732432692)
XLA Ops:
  5.8 5.5 %collective-permute-start = (bf16[2,3,16,64]{3,2,1,0:T(8,128)(2,1)}, bf16[2,3,16,64]{3,2,1,0:T(8,128)(2,1)}, u32[]{:S(2)}, u32[]{:S(2)}) collective-permute-start(bf16[2,3,16,64]{3,2,1,0:T(8,128)(2,1)} %bitcast_convert_fusion.1), channel_id=1, source_target_pairs={{0,1},{2,3},{4,5},{6,7},{8,9},{10,11},{12,13},{14,15},{16,17},{18,... | collective-permute-start | bytes 36872 | tf_op jit(solution)/shard_map/ppermute | solution.py:21
  16.9 1.5 gather_fusion.3
  20.0 1.5 gather_fusion.4
  22.6 4.5 %collective-permute-start.3 = (f32[3,16,64]{2,1,0:T(8,128)S(1)}, f32[3,16,64]{2,1,0:T(8,128)S(1)}, u32[]{:S(2)}, u32[]{:S(2)}) collective-permute-start(f32[3,16,64]{2,1,0:T(8,128)S(1)} %get-tuple-element.37), channel_id=1, source_target_pairs={{2,0},{4,2},{6,4},{8,6},{10,8},{12,10},{14,12},{16,14},{18,16},{20... | collective-permute-start | bytes 36872 | tf_op jit(solution)/shard_map/ppermute | solution.py:24
  29.1 2.2 %copy.262 = f32[3,3,8,256,1]{2,0,1,4,3:T(4,128)} copy(f32[3,3,8,256,1]{3,2,1,0,4:T(8,128)} %bitcast.118) | data formatting | bytes 147456 | tf_op args[5]
  33.4 2.1 %copy.237 = f32[2,3,16,512]{2,0,3,1:T(2,128)} copy(f32[2,3,16,512]{3,2,1,0:T(8,128)S(1)} %concatenate.18) | data formatting | bytes 393216 | tf_op jit(solution)/shard_map/concatenate | solution.py:78
  35.5 23.1 %gather_fusion = f32[2048,2,3,16]{3,1,2,0:T(2,128)} fusion(f32[2,3,16,512]{2,0,3,1:T(2,128)} %copy.237, s32[2048]{0:T(1024)S(1)} %broadcast_clamp_fusion), kind=kCustom, calls=%fused_computation.4 | custom fusion | bytes 1581056 | tf_op jit(solution)/shard_map/jit(_take)/gather | solution.py:79
  58.6 10.7 %fusion.6 = f32[256,2,16,3]{2,3,1,0:T(4,128)S(1)} fusion(f32[3,3,8,256,1]{2,0,1,4,3:T(4,128)} %copy.262, f32[8,256,2,3,16]{4,2,3,1,0:T(2,128)} %bitcast.110, pred[8,256]{0,1:T(8,128)(4,1)S(1)} %copy.228), kind=kOutput, calls=%fused_computation.12 | convolution fusion | flops 7274496 | bytes 960512 | tf_op jit(solution)/shard_map/cdkn,sdvkn->scvn/dot_general | solution.py:80
  71.7 2.1 %copy.241 = f32[2,2,3,16,256]{3,1,2,0,4:T(2,128)} copy(f32[2,2,3,16,256]{4,3,2,1,0:T(8,128)S(1)} %pad_maximum_fusion) | data formatting | bytes 393216 | tf_op jit(solution)/shard_map/stack | solution.py:92
  73.8 4.2 %reshape.173 = f32[16,1,3072]{2,1,0:T(1,128)} reshape(f32[256,2,3,2,16]{4,3,2,1,0:T(2,128)} %bitcast.111) | data formatting | bytes 393216
  78.0 3.7 %all-to-all-start = ((f32[16,1,3072]{2,1,0:T(1,128)}), f32[16,1,3072]{2,1,0:T(1,128)S(1)}, u32[]{:S(2)}, u32[]{:S(2)}) async-start(f32[16,1,3072]{2,1,0:T(1,128)} %reshape.173), calls=%async_computation | async-start | bytes 393216 | tf_op jit(solution)/shard_map/all_to_all | solution.py:95
  81.8 8.7 %all-to-all-done = f32[16,1,3072]{2,1,0:T(1,128)S(1)} async-done(((f32[16,1,3072]{2,1,0:T(1,128)}), f32[16,1,3072]{2,1,0:T(1,128)S(1)}, u32[]{:S(2)}, u32[]{:S(2)}) %all-to-all-start) | async-done | bytes 196640 | tf_op jit(solution)/shard_map/all_to_all | solution.py:95
  92.1 3.3 %reshape.174 = f32[256,2,3,2,16]{4,3,2,1,0:T(2,128)} reshape(f32[16,3072]{1,0:T(8,128)S(1)} %reduce) | data formatting | bytes 393216
  95.4 3.7 %copy.242 = f32[2,2,3,16,16,16]{5,3,2,1,4,0:T(8,128)} copy(f32[2,2,3,16,16,16]{3,1,2,0,5,4:T(2,128)} %bitcast.112) | data formatting | bytes 393216 | tf_op jit(solution)/shard_map/all_to_all | solution.py:95
  99.1 2.0 %copy.243 = f32[2,32,3,16,16]{1,4,3,2,0:T(8,128)S(1)} copy(f32[2,32,3,16,16]{4,3,2,1,0:T(8,128)} %bitcast.113) | data formatting | bytes 393216 | tf_op jit(solution)/shard_map/all_to_all | solution.py:95
  102.0 3.9 %slice_bitcast_fusion = (bf16[1,2,2,3,16,16]{1,5,4,3,2,0:T(8,128)(2,1)S(1)}, bf16[1,2,2,3,16,16]{1,5,4,3,2,0:T(8,128)(2,1)S(1)}, bf16[1,2,2,3,16,16]{1,5,4,3,2,0...) fusion(bf16[32,2,3,16,16]{0,4,3,2,1:T(8,128)(2,1)S(1)} %convert, ...), kind=kLoop, calls=%fused_computation.14 | loop fusion | bytes 196608 | tf_op jit(solution)/shard_map/stack | solution.py:107
  105.9 2.3 %copy.244 = bf16[1,2,2,3,16,16]{5,4,3,2,1,0:T(8,128)(2,1)} copy(bf16[1,2,2,3,16,16]{1,5,4,3,2,0:T(8,128)(2,1)} %get-tuple-element.29) | data formatting | bytes 12288 | tf_op jit(solution)/shard_map/stack | solution.py:107
  108.2 1.4 constant_dynamic-update-slice_fusion.15
  109.7 2.3 %copy.245 = bf16[1,2,2,3,16,16]{5,4,3,2,1,0:T(8,128)(2,1)} copy(bf16[1,2,2,3,16,16]{1,5,4,3,2,0:T(8,128)(2,1)} %get-tuple-element.28) | data formatting | bytes 12288 | tf_op jit(solution)/shard_map/stack | solution.py:107
  112.0 2.3 %copy.246 = bf16[1,2,2,3,16,16]{5,4,3,2,1,0:T(8,128)(2,1)} copy(bf16[1,2,2,3,16,16]{1,5,4,3,2,0:T(8,128)(2,1)} %get-tuple-element.27) | data formatting | bytes 12288 | tf_op jit(solution)/shard_map/stack | solution.py:107
  114.2 2.3 %copy.247 = bf16[1,2,2,3,16,16]{5,4,3,2,1,0:T(8,128)(2,1)} copy(bf16[1,2,2,3,16,16]{1,5,4,3,2,0:T(8,128)(2,1)} %get-tuple-element.26) | data formatting | bytes 12288 | tf_op jit(solution)/shard_map/stack | solution.py:107
  116.5 2.3 %copy.248 = bf16[1,2,2,3,16,16]{5,4,3,2,1,0:T(8,128)(2,1)} copy(bf16[1,2,2,3,16,16]{1,5,4,3,2,0:T(8,128)(2,1)} %get-tuple-element.25) | data formatting | bytes 12288 | tf_op jit(solution)/shard_map/stack | solution.py:107
  118.8 2.3 %copy.249 = bf16[1,2,2,3,16,16]{5,4,3,2,1,0:T(8,128)(2,1)} copy(bf16[1,2,2,3,16,16]{1,5,4,3,2,0:T(8,128)(2,1)} %get-tuple-element.24) | data formatting | bytes 12288 | tf_op jit(solution)/shard_map/stack | solution.py:107
  121.1 2.3 %copy.250 = bf16[1,2,2,3,16,16]{5,4,3,2,1,0:T(8,128)(2,1)} copy(bf16[1,2,2,3,16,16]{1,5,4,3,2,0:T(8,128)(2,1)} %get-tuple-element.23) | data formatting | bytes 12288 | tf_op jit(solution)/shard_map/stack | solution.py:107
  123.4 2.3 %copy.251 = bf16[1,2,2,3,16,16]{5,4,3,2,1,0:T(8,128)(2,1)} copy(bf16[1,2,2,3,16,16]{1,5,4,3,2,0:T(8,128)(2,1)} %get-tuple-element.22) | data formatting | bytes 12288 | tf_op jit(solution)/shard_map/stack | solution.py:107
  125.7 2.3 %copy.252 = bf16[1,2,2,3,16,16]{5,4,3,2,1,0:T(8,128)(2,1)} copy(bf16[1,2,2,3,16,16]{1,5,4,3,2,0:T(8,128)(2,1)} %get-tuple-element.21) | data formatting | bytes 12288 | tf_op jit(solution)/shard_map/stack | solution.py:107
  128.0 2.3 %copy.253 = bf16[1,2,2,3,16,16]{5,4,3,2,1,0:T(8,128)(2,1)} copy(bf16[1,2,2,3,16,16]{1,5,4,3,2,0:T(8,128)(2,1)} %get-tuple-element.20) | data formatting | bytes 12288 | tf_op jit(solution)/shard_map/stack | solution.py:107
  130.3 2.3 %copy.254 = bf16[1,2,2,3,16,16]{5,4,3,2,1,0:T(8,128)(2,1)} copy(bf16[1,2,2,3,16,16]{1,5,4,3,2,0:T(8,128)(2,1)} %get-tuple-element.19) | data formatting | bytes 12288 | tf_op jit(solution)/shard_map/stack | solution.py:107
  132.6 2.3 %copy.255 = bf16[1,2,2,3,16,16]{5,4,3,2,1,0:T(8,128)(2,1)} copy(bf16[1,2,2,3,16,16]{1,5,4,3,2,0:T(8,128)(2,1)} %get-tuple-element.18) | data formatting | bytes 12288 | tf_op jit(solution)/shard_map/stack | solution.py:107
  134.9 2.3 %copy.256 = bf16[1,2,2,3,16,16]{5,4,3,2,1,0:T(8,128)(2,1)} copy(bf16[1,2,2,3,16,16]{1,5,4,3,2,0:T(8,128)(2,1)} %get-tuple-element.17) | data formatting | bytes 12288 | tf_op jit(solution)/shard_map/stack | solution.py:107
  140.0 1.4 constant_dynamic-update-slice_fusion.14
  141.4 1.4 constant_dynamic-update-slice_fusion.13
  142.8 1.4 constant_dynamic-update-slice_fusion.12
  144.2 1.4 constant_dynamic-update-slice_fusion.11
  145.6 1.4 constant_dynamic-update-slice_fusion.10
  147.1 1.4 constant_dynamic-update-slice_fusion.9
  148.5 1.4 constant_dynamic-update-slice_fusion.8
  149.9 1.4 constant_dynamic-update-slice_fusion.7
  151.3 1.4 constant_dynamic-update-slice_fusion.6
  152.7 1.4 constant_dynamic-update-slice_fusion.5
  154.1 1.4 constant_dynamic-update-slice_fusion.4
  155.6 1.4 constant_dynamic-update-slice_fusion.3
  157.0 1.4 constant_dynamic-update-slice_fusion.2
  159.6 2.0 %reshape.175 = bf16[16,2,1536]{2,1,0:T(2,128)(2,1)S(1)} reshape(bf16[16,2,2,3,16,16]{5,4,3,2,1,0:T(8,128)(2,1)} %constant_dynamic-update-slice_fusion) | data formatting | bytes 196608
  161.6 10.0 %all_to_all.23 = bf16[16,2,1536]{2,1,0:T(2,128)(2,1)S(1)} all-to-all(bf16[16,2,1536]{2,1,0:T(2,128)(2,1)S(1)} %reshape.175), channel_id=1, replica_groups=mesh['wheel'=16,'slab'=2] {'wheel'}, dimensions={0} | all-to-all | bytes 196608 | tf_op jit(solution)/shard_map/all_to_all | solution.py:106
  172.1 1.4 copy.260
  173.5 1.7 reshape_reshape.3
  175.8 1.5 fusion.9
  (66 shorter events, 28.2 us)
Async XLA Ops:
  0.0 175.8 %copy-start = (bf16[1,8,384,384]{3,2,1,0:T(8,128)(2,1)S(1)}, bf16[1,8,384,384]{3,2,1,0:T(8,128)(2,1)}, u32[]{:S(2)}) copy-start(bf16[1,8,384,384]{3,2,1,0:T(8,128)(2,1)} %param.17) | copy-start | bytes 7077892
  0.0 27.1 %copy-start.1 = (f32[2,2,3,16,256]{4,3,2,1,0:T(8,128)S(1)}, f32[2,2,3,16,256]{4,3,2,1,0:T(8,128)}, u32[]{:S(2)}) copy-start(f32[2,2,3,16,256]{4,3,2,1,0:T(8,128)} %param.10) | copy-start | bytes 589828
  0.0 27.1 %copy-start.2 = (s32[8,256]{1,0:T(8,128)S(1)}, s32[8,256]{1,0:T(8,128)}, u32[]{:S(2)}) copy-start(s32[8,256]{1,0:T(8,128)} %param.12) | copy-start | bytes 24580
  0.0 27.7 %copy-start.3 = (f32[3,256]{1,0:T(4,128)S(1)}, f32[3,256]{1,0:T(4,128)}, u32[]{:S(2)}) copy-start(f32[3,256]{1,0:T(4,128)} %param.16) | copy-start | bytes 9220
  5.8 25.7 %collective-permute-start = (bf16[2,3,16,64]{3,2,1,0:T(8,128)(2,1)}, bf16[2,3,16,64]{3,2,1,0:T(8,128)(2,1)}, u32[]{:S(2)}, u32[]{:S(2)}) collective-permute-start(bf16[2,3,16,64]{3,2,1,0:T(8,128)(2,1)} %bitcast_convert_fusion.1), channel_id=1, source_target_pairs={{0,1},{2,3},{4,5},{6,7},{8,9},{10,11},{12,13},{14,15},{16,17},{18,... | collective-permute-start | bytes 36872 | tf_op jit(solution)/shard_map/ppermute | solution.py:21
  14.8 16.7 %collective-permute-start.1 = (bf16[2,3,16,64]{3,2,1,0:T(8,128)(2,1)}, bf16[2,3,16,64]{3,2,1,0:T(8,128)(2,1)}, u32[]{:S(2)}, u32[]{:S(2)}) collective-permute-start(bf16[2,3,16,64]{3,2,1,0:T(8,128)(2,1)} %bitcast_convert_fusion), channel_id=1, source_target_pairs={{1,0},{3,2},{5,4},{7,6},{9,8},{11,10},{13,12},{15,14},{17,16},{19,... | collective-permute-start | bytes 36872 | tf_op jit(solution)/shard_map/ppermute | solution.py:24
  20.0 12.5 %collective-permute-start.2 = (f32[3,16,64]{2,1,0:T(8,128)}, f32[3,16,64]{2,1,0:T(8,128)}, u32[]{:S(2)}, u32[]{:S(2)}) collective-permute-start(f32[3,16,64]{2,1,0:T(8,128)} %get-tuple-element.38), channel_id=1, source_target_pairs={{0,2},{2,4},{4,6},{6,8},{8,10},{10,12},{12,14},{14,16},{16,18},{18... | collective-permute-start | bytes 36872 | tf_op jit(solution)/shard_map/ppermute | solution.py:21
  22.6 10.7 %collective-permute-start.3 = (f32[3,16,64]{2,1,0:T(8,128)S(1)}, f32[3,16,64]{2,1,0:T(8,128)S(1)}, u32[]{:S(2)}, u32[]{:S(2)}) collective-permute-start(f32[3,16,64]{2,1,0:T(8,128)S(1)} %get-tuple-element.37), channel_id=1, source_target_pairs={{2,0},{4,2},{6,4},{8,6},{10,8},{12,10},{14,12},{16,14},{18,16},{20... | collective-permute-start | bytes 36872 | tf_op jit(solution)/shard_map/ppermute | solution.py:24
  78.0 12.5 %all-to-all-start = ((f32[16,1,3072]{2,1,0:T(1,128)}), f32[16,1,3072]{2,1,0:T(1,128)S(1)}, u32[]{:S(2)}, u32[]{:S(2)}) async-start(f32[16,1,3072]{2,1,0:T(1,128)} %reshape.173), calls=%async_computation | async-start | bytes 393216 | tf_op jit(solution)/shard_map/all_to_all | solution.py:95
